TPU v7x, 32 devices: a whole 2x2x4 slice. The times are simulated.
32 devices in a mesh: groups: 2 (over x), inner: 16 (over z, y, core).
Axes of the slice: x: 2, y: 2, z: 4, core: 2. Of those that a mesh axis runs over, the one named last changes fastest.
Arguments:
- hidden_rows: bfloat16 [2048, 2048], P(('groups', 'inner')), parts along dimension 0, may hold values from -6 to 6
- token_embed: bfloat16 [2048, 2048], P(('groups', 'inner')), parts along dimension 0, may hold values from -6 to 6
- first_routes: int32 [2048, 8], P(('groups', 'inner')), parts along dimension 0, may hold values from 0 to 15, all different within a row; in each aligned block of 64 rows (0 to 63, 64 to 127, ...) at most 48 rows name the same one
- first_gates: float32 [2048, 8], P(('groups', 'inner')), parts along dimension 0, may hold values from 0.2 to 0.6
- first_gate_up: bfloat16 [16, 2048, 1024], P('inner'), may hold values from -0.125 to 0.125
- first_down: bfloat16 [16, 512, 2048], P('inner'), may hold values from -0.25 to 0.25
- second_routes: int32 [2048, 8], P(('groups', 'inner')), parts along dimension 0, may hold values from 0 to 15, all different within a row; in each aligned block of 64 rows (0 to 63, 64 to 127, ...) at most 48 rows name the same one
- second_gates: float32 [2048, 8], P(('groups', 'inner')), parts along dimension 0, may hold values from 0.2 to 0.6
- second_gate_up: bfloat16 [16, 2048, 1024], P('inner'), may hold values from -0.125 to 0.125
- second_down: bfloat16 [16, 512, 2048], P('inner'), may hold values from -0.25 to 0.25
- hidden_gain: float32 [2048], replicated, may hold values from 0.25 to 1.75
- embed_gain: float32 [2048], replicated, may hold values from 0.25 to 1.75
- merge_weight: bfloat16 [4096, 2048], P('inner'), may hold values from -0.09375 to 0.09375
Outputs:
- final_rows: bfloat16 [2048, 2048], P(('groups', 'inner')), parts along dimension 0
There are 2 independent parts, one for each index of `groups`. A program takes and returns all parts, laid end to end along the dimension named above; an argument that names none is the same for every part. Nothing has to cross between parts.
Inputs may be any that keep to these rules, and one draw needn't show every extreme that they name: `first_routes`: among the 64 tokens of one block, no expert is named more than 48 times, and in every draw some expert is named exactly 48 times in some block. `second_routes`: among the 64 tokens of one block, no expert is named more than 48 times, and in every draw some expert is named exactly 48 times in some block.
All inputs are finite; a program needn't handle non-finite values.
Results may differ from a plain program's by a relative error of at most 0.01.
Values may be sent and summed in bfloat16 or wider, within the bound.
A program may use at most 128 MiB of HBM per device.

v0:
```python
import jax
import jax.numpy as jnp
from jax import lax
from jax.sharding import PartitionSpec as P

EPSILON = 1e-06


def rms_scale(values, gain_vec):
    widened = values.astype(jnp.float32)
    inverse_rms = lax.rsqrt(jnp.mean(widened * widened, axis=-1, keepdims=True) + EPSILON)
    return (widened * inverse_rms * gain_vec).astype(jnp.bfloat16)


def dense_gates(routes, gates, experts):
    hit = routes[:, :, None] == jnp.arange(experts, dtype=jnp.int32)[None, None, :]
    return jnp.sum(jnp.where(hit, gates[:, :, None], 0.0), axis=1)


def dense_layer(rows, gate_column, gate_up, down):
    everyone = lax.all_gather(rows, "inner", axis=0, tiled=True)
    width = down.shape[0]
    projected = jnp.dot(everyone, gate_up, preferred_element_type=jnp.float32)
    inner = (jax.nn.silu(projected[:, :width]) * projected[:, width:]).astype(jnp.bfloat16)
    out = jnp.dot(inner, down, preferred_element_type=jnp.float32)
    share = jnp.where(gate_column > 0, out * gate_column, 0.0).astype(jnp.bfloat16)
    return lax.psum_scatter(share, "inner", scatter_dimension=0, tiled=True).astype(jnp.float32)


def local(
    hidden_rows,
    token_embed,
    first_routes,
    first_gates,
    first_gate_up,
    first_down,
    second_routes,
    second_gates,
    second_gate_up,
    second_down,
    hidden_gain,
    embed_gain,
    merge_weight,
):
    experts = lax.axis_size("inner")
    me = lax.axis_index("inner")
    both = jnp.concatenate(
        [
            dense_gates(first_routes, first_gates, experts),
            dense_gates(second_routes, second_gates, experts),
        ],
        axis=1,
    )
    both = lax.all_gather(both, "inner", axis=0, tiled=True)
    first_column = lax.dynamic_slice_in_dim(both, me, 1, axis=1)
    second_column = lax.dynamic_slice_in_dim(both, me + experts, 1, axis=1)
    first_moe = dense_layer(hidden_rows, first_column, first_gate_up[0], first_down[0])
    after_first = (hidden_rows.astype(jnp.float32) + first_moe).astype(jnp.bfloat16)
    merged_in = jnp.concatenate(
        [rms_scale(after_first, hidden_gain), rms_scale(token_embed, embed_gain)], axis=1
    )
    columns = lax.all_to_all(merged_in, "inner", split_axis=1, concat_axis=0, tiled=True)
    partial = jnp.dot(columns, merge_weight, preferred_element_type=jnp.float32)
    merged = lax.psum_scatter(
        partial.astype(jnp.bfloat16), "inner", scatter_dimension=0, tiled=True
    ).astype(jnp.float32)
    after_merge = (after_first.astype(jnp.float32) + jax.nn.silu(merged)).astype(jnp.bfloat16)
    second_moe = dense_layer(after_merge, second_column, second_gate_up[0], second_down[0])
    return (after_merge.astype(jnp.float32) + second_moe).astype(jnp.bfloat16)


def solution(mesh):
    rows = P(("groups", "inner"), None)
    return jax.shard_map(
        local,
        mesh=mesh,
        in_specs=(
            rows,
            rows,
            rows,
            rows,
            P("inner", None, None),
            P("inner", None, None),
            rows,
            rows,
            P("inner", None, None),
            P("inner", None, None),
            P(),
            P(),
            P("inner", None),
        ),
        out_specs=rows,
        check_vma=False,
    )
```

profile of v0, /device:TPU:0, one launch (start us, length us, event | category | flops | bytes accessed | tf_op | source)
XLA Modules:
  0.0 384.9 jit_solution(18183789587168572780)
XLA Ops:
  6.5 0.7 all-gather.4.cloned.1.call-update
  7.3 0.8 select_reduce_fusion
  8.1 24.3 %all-gather = f32[16,64,32]{1,2,0:T(8,128)S(1)} all-gather(f32[1,64,32]{1,2,0:T(8,128)S(1)} %maximum_bitcast_fusion), channel_id=1, replica_groups=mesh['groups'=2,'inner'=16] {'inner'}, dimensions={0}, use_global_device_ids=true | all-gather | bytes 139264 | tf_op jit(solution)/shard_map/all_gather | solution.py:54
  32.3 0.2 copy.34
  32.5 0.1 reshape.26
  32.7 30.4 %all-gather.4.cloned.1.call-done = bf16[1024,2048]{1,0:T(8,128)(2,1)} async-done(((bf16[64,2048]{1,0:T(8,128)(2,1)}), bf16[1024,2048]{1,0:T(8,128)(2,1)}) %all-gather.4.cloned.1.call-update) | async-done | bytes 4194320 | tf_op jit(solution)/shard_map/all_gather | solution.py:21
  63.1 7.5 %fusion.2 = f32[1024,1024]{1,0:T(8,128)S(1)} fusion(bf16[1024,2048]{1,0:T(8,128)(2,1)} %all-gather.4.cloned.1.call-done, bf16[1,2048,1024]{2,1,0:T(8,128)(2,1)} %param.17), kind=kOutput, calls=%fused_computation.4 | convolution fusion | flops 4294967296 | bytes 12582912 | tf_op jit(solution)/shard_map/dot_general | solution.py:23
  70.6 4.1 %select_convert_fusion.1 = bf16[1024,2048]{1,0:T(8,128)(2,1)} fusion(f32[1024]{0:T(1024)S(1)} %bitcast.33, pred[1024]{0:T(1024)(128)(4,1)S(1)} %get-tuple-element.5, bf16[1,512,2048]{2,1,0:T(8,128)(2,1)S(1)} %copy-done, f32[1024,1024]{1,0:T(8,128)S(1)} %fusion.2), kind=kOutput, calls=%fused_computation.1 | convolution fusion | flops 2156920832 | bytes 10490880 | tf_op jit(solution)/shard_map/dot_general | solution.py:25
  74.8 0.9 copy-done.4
  75.7 0.2 fusion.12
  75.8 0.1 fusion.14
  76.0 70.2 %reduce-scatter.4.cloned.1.call-done = bf16[64,2048]{1,0:T(8,128)(2,1)} async-done(((bf16[1024,2048]{1,0:T(8,128)(2,1)}), bf16[64,2048]{1,0:T(8,128)(2,1)}) %reduce-scatter.4.cloned.1.call-update) | async-done | bytes 262160 | tf_op jit(solution)/shard_map/reduce_scatter | solution.py:27
  146.2 1.2 fusion.18
  147.5 1.1 fusion.20
  148.7 17.8 %all_to_all.19 = bf16[64,16,256]{2,0,1:T(8,128)(2,1)S(1)} all-to-all(bf16[64,16,256]{2,0,1:T(8,128)(2,1)S(1)} %bitcast.31), channel_id=1, replica_groups=mesh['groups'=2,'inner'=16] {'inner'}, dimensions={1} | all-to-all | bytes 1048576 | tf_op jit(solution)/shard_map/all_to_all | solution.py:62
  166.5 3.2 convolution_convert_fusion
  169.7 0.0 all-gather.6.cloned.1.call-start
  169.7 72.4 %reduce-scatter.6.cloned.1.call-done = bf16[64,2048]{1,0:T(8,128)(2,1)} async-done(((bf16[1024,2048]{1,0:T(8,128)(2,1)}), bf16[64,2048]{1,0:T(8,128)(2,1)}) %reduce-scatter.6.cloned.1.call-update) | async-done | bytes 262160 | tf_op jit(solution)/shard_map/reduce_scatter | solution.py:64
  242.1 1.8 fusion.21
  244.0 49.4 %all-gather.6.cloned.1.call-done = bf16[1024,2048]{1,0:T(8,128)(2,1)} async-done(((bf16[64,2048]{1,0:T(8,128)(2,1)}), bf16[1024,2048]{1,0:T(8,128)(2,1)}) %all-gather.6.cloned.1.call-update) | async-done | bytes 4194320 | tf_op jit(solution)/shard_map/all_gather | solution.py:21
  293.5 7.6 %fusion = f32[1024,1024]{1,0:T(8,128)S(1)} fusion(bf16[1024,2048]{1,0:T(8,128)(2,1)} %all-gather.6.cloned.1.call-done, bf16[1,2048,1024]{2,1,0:T(8,128)(2,1)} %param.21), kind=kOutput, calls=%fused_computation.2 | convolution fusion | flops 4294967296 | bytes 12582912 | tf_op jit(solution)/shard_map/dot_general | solution.py:23
  301.1 4.1 %select_convert_fusion = bf16[1024,2048]{1,0:T(8,128)(2,1)} fusion(f32[1024]{0:T(1024)S(1)} %bitcast.32, pred[1024]{0:T(1024)(128)(4,1)S(1)} %get-tuple-element.9, bf16[1,512,2048]{2,1,0:T(8,128)(2,1)S(1)} %copy-done.8, f32[1024,1024]{1,0:T(8,128)S(1)} %fusion), kind=kOutput, calls=%fused_computation | convolution fusion | flops 2156920832 | bytes 10490880 | tf_op jit(solution)/shard_map/dot_general | solution.py:25
  305.2 71.4 %reduce-scatter.8.cloned.1.call-done = bf16[64,2048]{1,0:T(8,128)(2,1)} async-done(((bf16[1024,2048]{1,0:T(8,128)(2,1)}), bf16[64,2048]{1,0:T(8,128)(2,1)}) %reduce-scatter.8.cloned.1.call-update) | async-done | bytes 262160 | tf_op jit(solution)/shard_map/reduce_scatter | solution.py:27
  376.7 1.7 add_convert_fusion
  (31 shorter events, 0.4 us)
Async XLA Ops:
  6.5 64.1 %copy-start = (bf16[1,512,2048]{2,1,0:T(8,128)(2,1)S(1)}, bf16[1,512,2048]{2,1,0:T(8,128)(2,1)}, u32[]{:S(2)}) copy-start(bf16[1,512,2048]{2,1,0:T(8,128)(2,1)} %param.18) | copy-start | bytes 6291460
  6.5 56.6 %all-gather.4.cloned.1.call-start = ((), (), s32[]{:S(2)}) async-start(), calls=%async_computation.4 | async-start | bytes 4456448 | tf_op jit(solution)/shard_map/all_gather | solution.py:21
  7.3 139.0 %reduce-scatter.4.cloned.1.call-start = ((), (), s32[]{:S(2)}) async-start(), calls=%async_computation.5 | async-start | bytes 4456448 | tf_op jit(solution)/shard_map/reduce_scatter | solution.py:27
  74.7 0.9 copy-start.4
  74.7 1.1 copy-start.6
  74.7 71.5 %copy-start.1 = (bf16[64,2048]{1,0:T(8,128)(2,1)S(1)}, bf16[64,2048]{1,0:T(8,128)(2,1)}, u32[]{:S(2)}) copy-start(bf16[64,2048]{1,0:T(8,128)(2,1)} %param.13) | copy-start | bytes 786436
  74.7 72.7 %copy-start.7 = (f32[2048]{0:T(1024)S(1)}, f32[2048]{0:T(1024)}, u32[]{:S(2)}) copy-start(f32[2048]{0:T(1024)} %param.23) | copy-start | bytes 24580
  74.8 167.4 %reduce-scatter.6.cloned.1.call-start = ((), (), s32[]{:S(2)}) async-start(), calls=%async_computation.6 | async-start | bytes 4456448 | tf_op jit(solution)/shard_map/reduce_scatter | solution.py:64
  146.2 20.3 %copy-start.5 = (bf16[256,2048]{1,0:T(8,128)(2,1)S(1)}, bf16[256,2048]{1,0:T(8,128)(2,1)}, u32[]{:S(2)}) copy-start(bf16[256,2048]{1,0:T(8,128)(2,1)} %param.25) | copy-start | bytes 3145732
  166.5 75.6 %copy-start.3 = (bf16[64,2048]{1,0:T(8,128)(2,1)S(1)}, bf16[64,2048]{1,0:T(8,128)(2,1)}, u32[]{:S(2)}) copy-start(bf16[64,2048]{1,0:T(8,128)(2,1)} %reduce-scatter.4.cloned.1.call-done) | copy-start | bytes 786436
  169.7 123.8 %all-gather.6.cloned.1.call-start = ((), (), s32[]{:S(2)}) async-start(), calls=%async_computation.7 | async-start | bytes 4456448 | tf_op jit(solution)/shard_map/all_gather | solution.py:21
  244.0 132.7 %reduce-scatter.8.cloned.1.call-start = ((), (), s32[]{:S(2)}) async-start(), calls=%async_computation.8 | async-start | bytes 4456448 | tf_op jit(solution)/shard_map/reduce_scatter | solution.py:27
  293.5 7.7 %copy-start.8 = (bf16[1,512,2048]{2,1,0:T(8,128)(2,1)S(1)}, bf16[1,512,2048]{2,1,0:T(8,128)(2,1)}, u32[]{:S(2)}) copy-start(bf16[1,512,2048]{2,1,0:T(8,128)(2,1)} %param.22) | copy-start | bytes 6291460
  305.2 71.5 %copy-start.2 = (bf16[64,2048]{1,0:T(8,128)(2,1)S(1)}, bf16[64,2048]{1,0:T(8,128)(2,1)}, u32[]{:S(2)}) copy-start(bf16[64,2048]{1,0:T(8,128)(2,1)} %fusion.21) | copy-start | bytes 786436
Sparse Core Ops, SparseCore 0:
  9.5 53.5 all-gather.3
  74.9 71.2 reduce-scatter.3
  169.8 72.2 reduce-scatter.5
  244.1 49.2 all-gather.5
  305.4 71.2 reduce-scatter.7
where the time goes:
time: 385 us
  waiting for transfers between devices  295 us (77%)
  blocking collectives  42.1 us (11%)
  matrix products  26.5 us (7%)
  between operations  13.2 us (3%)
  other arithmetic  7.03 us (2%)
    reduce_scatter x2, waiting for transfers between devices, dense_layer(): lax.psum_scatter(share, 'inner', scatter_dimension=0, tiled=True)  142 us
    all_gather x2, waiting for transfers between devices, dense_layer(): everyone = lax.all_gather(rows, 'inner', axis=0, tiled=True)  79.8 us
    reduce_scatter x1, waiting for transfers between devices, local(): lax.psum_scatter(partial.astype(jnp.bfloat16), 'inner', scatter_dimension...  72.4 us
    all_gather x1, blocking collectives, local(): both = lax.all_gather(both, 'inner', axis=0, tiled=True)  24.3 us
    all_to_all x1, blocking collectives, local(): lax.all_to_all(merged_in, 'inner', split_axis=1, concat_axis=0, tiled=True)  17.8 us
    dot_general x2, matrix products, dense_layer(): projected = jnp.dot(everyone, gate_up, preferred_element_type=jnp.float32)  15.1 us
    dot_general x2, matrix products, dense_layer(): out = jnp.dot(inner, down, preferred_element_type=jnp.float32)  8.21 us
  transfers between devices with their start and end apart: 5, of which 5 were waited for; matrix products, arithmetic and copies ran while one was open for 0% of the time, Pallas kernels for 0%

commit v1 on v0

--- a/solution.py
+++ b/solution.py
@@ -18,7 +18,13 @@
 
 
 def dense_layer(rows, gate_column, gate_up, down):
-    everyone = lax.all_gather(rows, "inner", axis=0, tiled=True)
+    devices = lax.axis_size("inner")
+    held, tiles = (rows, [rows])
+    for _ in range(devices - 1):
+        held = lax.ppermute(held, "inner", [(i, (i + 1) % devices) for i in range(devices)])
+        tiles.insert(0, held)
+    line = jnp.concatenate(tiles, axis=0)
+    everyone = jnp.roll(line, (lax.axis_index("inner") + 1) * rows.shape[0], axis=0)
     width = down.shape[0]
     projected = jnp.dot(everyone, gate_up, preferred_element_type=jnp.float32)
     inner = (jax.nn.silu(projected[:, :width]) * projected[:, width:]).astype(jnp.bfloat16)

time: 385 us -> 556 us (1.44)
  waiting for transfers between devices: 295 us -> 459 us
  local copies, waits for them, and re-layouts: 1.22 us -> 16.3 us
    ppermute x0 -> x30, waiting for transfers between devices: none -> 246 us  [dense_layer(): lax.ppermute(held, 'inner', [(i, (i + 1) % devices) for i in range(device...]
    all_gather x2 -> x0, waiting for transfers between devices: 79.8 us -> none  [dense_layer(): everyone = lax.all_gather(rows, 'inner', axis=0, tiled=True)]
    unnamed x19 -> x79, local copies, waits for them, and re-layouts: 1.02 us -> 16.1 us
  transfers between devices with their start and end apart: 5 -> 33, of which waited for: 5 -> 32; matrix products, arithmetic and copies ran while one was open for 0% -> 0% of each run, Pallas kernels for 0% -> 0%
where the time goes in v1:
time: 556 us; the launch traced here: 555 us
  waiting for transfers between devices  459 us (83%)
  blocking collectives  36.8 us (7%)
  matrix products  22.7 us (4%)
  local copies, waits for them, and re-layouts  16.3 us (3%)
  between operations  13.6 us (2%)
  other arithmetic  6.39 us (1%)
    ppermute x30, waiting for transfers between devices, dense_layer(): lax.ppermute(held, 'inner', [(i, (i + 1) % devices) for i in range(device...  246 us
    reduce_scatter x2, waiting for transfers between devices, dense_layer(): lax.psum_scatter(share, 'inner', scatter_dimension=0, tiled=True)  140 us
    reduce_scatter x1, waiting for transfers between devices, local(): lax.psum_scatter(partial.astype(jnp.bfloat16), 'inner', scatter_dimension...  72.5 us
    all_gather x1, blocking collectives, local(): both = lax.all_gather(both, 'inner', axis=0, tiled=True)  19 us
    all_to_all x1, blocking collectives, local(): lax.all_to_all(merged_in, 'inner', split_axis=1, concat_axis=0, tiled=True)  17.8 us
    unnamed x79, local copies, waits for them, and re-layouts  16.1 us
    dot_general x2, matrix products, dense_layer(): projected = jnp.dot(everyone, gate_up, preferred_element_type=jnp.float32)  11.2 us
  transfers between devices with their start and end apart: 33, of which 32 were waited for; matrix products, arithmetic and copies ran while one was open for 0% of the time, Pallas kernels for 0%

profile of v1, /device:TPU:0, one launch (start us, length us, event | category | flops | bytes accessed | tf_op | source)
XLA Modules:
  0.0 555.5 jit_solution(3511299859143148977)
XLA Ops:
  7.0 9.2 %collective-permute-done = bf16[64,2048]{1,0:T(8,128)(2,1)S(1)} collective-permute-done((bf16[64,2048]{1,0:T(8,128)(2,1)}, bf16[64,2048]{1,0:T(8,128)(2,1)S(1)}, u32[]{:S(2)}, u32[]{:S(2)}) %collective-permute-start) | collective-permute-done | bytes 262176 | tf_op jit(solution)/shard_map/ppermute | solution.py:24
  33.3 8.5 %collective-permute-done.3 = bf16[64,2048]{1,0:T(8,128)(2,1)S(1)} collective-permute-done((bf16[64,2048]{1,0:T(8,128)(2,1)S(1)}, bf16[64,2048]{1,0:T(8,128)(2,1)S(1)}, u32[]{:S(2)}, u32[]{:S(2)}) %collective-permute-start.3) | collective-permute-done | bytes 262176 | tf_op jit(solution)/shard_map/ppermute | solution.py:24
  42.5 8.5 %collective-permute-done.4 = bf16[64,2048]{1,0:T(8,128)(2,1)S(1)} collective-permute-done((bf16[64,2048]{1,0:T(8,128)(2,1)S(1)}, bf16[64,2048]{1,0:T(8,128)(2,1)S(1)}, u32[]{:S(2)}, u32[]{:S(2)}) %collective-permute-start.4) | collective-permute-done | bytes 262176 | tf_op jit(solution)/shard_map/ppermute | solution.py:24
  51.7 8.5 %collective-permute-done.5 = bf16[64,2048]{1,0:T(8,128)(2,1)S(1)} collective-permute-done((bf16[64,2048]{1,0:T(8,128)(2,1)S(1)}, bf16[64,2048]{1,0:T(8,128)(2,1)S(1)}, u32[]{:S(2)}, u32[]{:S(2)}) %collective-permute-start.5) | collective-permute-done | bytes 262176 | tf_op jit(solution)/shard_map/ppermute | solution.py:24
  60.9 8.5 %collective-permute-done.6 = bf16[64,2048]{1,0:T(8,128)(2,1)S(1)} collective-permute-done((bf16[64,2048]{1,0:T(8,128)(2,1)S(1)}, bf16[64,2048]{1,0:T(8,128)(2,1)S(1)}, u32[]{:S(2)}, u32[]{:S(2)}) %collective-permute-start.6) | collective-permute-done | bytes 262176 | tf_op jit(solution)/shard_map/ppermute | solution.py:24
  70.1 8.5 %collective-permute-done.7 = bf16[64,2048]{1,0:T(8,128)(2,1)S(1)} collective-permute-done((bf16[64,2048]{1,0:T(8,128)(2,1)S(1)}, bf16[64,2048]{1,0:T(8,128)(2,1)S(1)}, u32[]{:S(2)}, u32[]{:S(2)}) %collective-permute-start.7) | collective-permute-done | bytes 262176 | tf_op jit(solution)/shard_map/ppermute | solution.py:24
  79.2 8.5 %collective-permute-done.8 = bf16[64,2048]{1,0:T(8,128)(2,1)S(1)} collective-permute-done((bf16[64,2048]{1,0:T(8,128)(2,1)S(1)}, bf16[64,2048]{1,0:T(8,128)(2,1)S(1)}, u32[]{:S(2)}, u32[]{:S(2)}) %collective-permute-start.8) | collective-permute-done | bytes 262176 | tf_op jit(solution)/shard_map/ppermute | solution.py:24
  88.4 8.5 %collective-permute-done.9 = bf16[64,2048]{1,0:T(8,128)(2,1)S(1)} collective-permute-done((bf16[64,2048]{1,0:T(8,128)(2,1)S(1)}, bf16[64,2048]{1,0:T(8,128)(2,1)S(1)}, u32[]{:S(2)}, u32[]{:S(2)}) %collective-permute-start.9) | collective-permute-done | bytes 262176 | tf_op jit(solution)/shard_map/ppermute | solution.py:24
  97.6 8.5 %collective-permute-done.10 = bf16[64,2048]{1,0:T(8,128)(2,1)S(1)} collective-permute-done((bf16[64,2048]{1,0:T(8,128)(2,1)S(1)}, bf16[64,2048]{1,0:T(8,128)(2,1)S(1)}, u32[]{:S(2)}, u32[]{:S(2)}) %collective-permute-start.10) | collective-permute-done | bytes 262176 | tf_op jit(solution)/shard_map/ppermute | solution.py:24
  116.0 8.5 %collective-permute-done.12 = bf16[64,2048]{1,0:T(8,128)(2,1)S(1)} collective-permute-done((bf16[64,2048]{1,0:T(8,128)(2,1)S(1)}, bf16[64,2048]{1,0:T(8,128)(2,1)S(1)}, u32[]{:S(2)}, u32[]{:S(2)}) %collective-permute-start.12) | collective-permute-done | bytes 262176 | tf_op jit(solution)/shard_map/ppermute | solution.py:24
  133.1 19.0 %all-gather = f32[16,64,32]{1,2,0:T(8,128)S(1)} all-gather(f32[1,64,32]{1,2,0:T(8,128)S(1)} %maximum_bitcast_fusion), channel_id=1, replica_groups=mesh['groups'=2,'inner'=16] {'inner'}, dimensions={0}, use_global_device_ids=true | all-gather | bytes 139264 | tf_op jit(solution)/shard_map/all_gather | solution.py:60
  172.2 70.1 %reduce-scatter.4.cloned.1.call-done = bf16[64,2048]{1,0:T(8,128)(2,1)} async-done(((bf16[1024,2048]{1,0:T(8,128)(2,1)}), bf16[64,2048]{1,0:T(8,128)(2,1)}) %reduce-scatter.4.cloned.1.call-update) | async-done | bytes 262160 | tf_op jit(solution)/shard_map/reduce_scatter | solution.py:33
  244.7 17.8 %all_to_all.19 = bf16[64,16,256]{2,0,1:T(8,128)(2,1)S(1)} all-to-all(bf16[64,16,256]{2,0,1:T(8,128)(2,1)S(1)} %bitcast.29), channel_id=1, replica_groups=mesh['groups'=2,'inner'=16] {'inner'}, dimensions={1} | all-to-all | bytes 1048576 | tf_op jit(solution)/shard_map/all_to_all | solution.py:68
  265.8 72.5 %reduce-scatter.6.cloned.1.call-done = bf16[64,2048]{1,0:T(8,128)(2,1)} async-done(((bf16[1024,2048]{1,0:T(8,128)(2,1)}), bf16[64,2048]{1,0:T(8,128)(2,1)}) %reduce-scatter.6.cloned.1.call-update) | async-done | bytes 262160 | tf_op jit(solution)/shard_map/reduce_scatter | solution.py:70
  348.0 8.5 %collective-permute-done.16 = bf16[64,2048]{1,0:T(8,128)(2,1)S(1)} collective-permute-done((bf16[64,2048]{1,0:T(8,128)(2,1)S(1)}, bf16[64,2048]{1,0:T(8,128)(2,1)S(1)}, u32[]{:S(2)}, u32[]{:S(2)}) %collective-permute-start.16) | collective-permute-done | bytes 262176 | tf_op jit(solution)/shard_map/ppermute | solution.py:24
  356.5 8.5 %collective-permute-done.17 = bf16[64,2048]{1,0:T(8,128)(2,1)S(1)} collective-permute-done((bf16[64,2048]{1,0:T(8,128)(2,1)S(1)}, bf16[64,2048]{1,0:T(8,128)(2,1)S(1)}, u32[]{:S(2)}, u32[]{:S(2)}) %collective-permute-start.17) | collective-permute-done | bytes 262176 | tf_op jit(solution)/shard_map/ppermute | solution.py:24
  365.0 8.5 %collective-permute-done.18 = bf16[64,2048]{1,0:T(8,128)(2,1)S(1)} collective-permute-done((bf16[64,2048]{1,0:T(8,128)(2,1)S(1)}, bf16[64,2048]{1,0:T(8,128)(2,1)S(1)}, u32[]{:S(2)}, u32[]{:S(2)}) %collective-permute-start.18) | collective-permute-done | bytes 262176 | tf_op jit(solution)/shard_map/ppermute | solution.py:24
  390.5 8.5 %collective-permute-done.21 = bf16[64,2048]{1,0:T(8,128)(2,1)S(1)} collective-permute-done((bf16[64,2048]{1,0:T(8,128)(2,1)S(1)}, bf16[64,2048]{1,0:T(8,128)(2,1)S(1)}, u32[]{:S(2)}, u32[]{:S(2)}) %collective-permute-start.21) | collective-permute-done | bytes 262176 | tf_op jit(solution)/shard_map/ppermute | solution.py:24
  399.0 8.5 %collective-permute-done.22 = bf16[64,2048]{1,0:T(8,128)(2,1)S(1)} collective-permute-done((bf16[64,2048]{1,0:T(8,128)(2,1)S(1)}, bf16[64,2048]{1,0:T(8,128)(2,1)S(1)}, u32[]{:S(2)}, u32[]{:S(2)}) %collective-permute-start.22) | collective-permute-done | bytes 262176 | tf_op jit(solution)/shard_map/ppermute | solution.py:24
  407.4 8.5 %collective-permute-done.23 = bf16[64,2048]{1,0:T(8,128)(2,1)S(1)} collective-permute-done((bf16[64,2048]{1,0:T(8,128)(2,1)S(1)}, bf16[64,2048]{1,0:T(8,128)(2,1)S(1)}, u32[]{:S(2)}, u32[]{:S(2)}) %collective-permute-start.23) | collective-permute-done | bytes 262176 | tf_op jit(solution)/shard_map/ppermute | solution.py:24
  415.9 8.5 %collective-permute-done.24 = bf16[64,2048]{1,0:T(8,128)(2,1)S(1)} collective-permute-done((bf16[64,2048]{1,0:T(8,128)(2,1)S(1)}, bf16[64,2048]{1,0:T(8,128)(2,1)S(1)}, u32[]{:S(2)}, u32[]{:S(2)}) %collective-permute-start.24) | collective-permute-done | bytes 262176 | tf_op jit(solution)/shard_map/ppermute | solution.py:24
  424.4 8.5 %collective-permute-done.25 = bf16[64,2048]{1,0:T(8,128)(2,1)S(1)} collective-permute-done((bf16[64,2048]{1,0:T(8,128)(2,1)S(1)}, bf16[64,2048]{1,0:T(8,128)(2,1)S(1)}, u32[]{:S(2)}, u32[]{:S(2)}) %collective-permute-start.25) | collective-permute-done | bytes 262176 | tf_op jit(solution)/shard_map/ppermute | solution.py:24
  432.9 8.5 %collective-permute-done.26 = bf16[64,2048]{1,0:T(8,128)(2,1)S(1)} collective-permute-done((bf16[64,2048]{1,0:T(8,128)(2,1)S(1)}, bf16[64,2048]{1,0:T(8,128)(2,1)S(1)}, u32[]{:S(2)}, u32[]{:S(2)}) %collective-permute-start.26) | collective-permute-done | bytes 262176 | tf_op jit(solution)/shard_map/ppermute | solution.py:24
  477.1 70.2 %reduce-scatter.8.cloned.1.call-done = bf16[64,2048]{1,0:T(8,128)(2,1)} async-done(((bf16[1024,2048]{1,0:T(8,128)(2,1)}), bf16[64,2048]{1,0:T(8,128)(2,1)}) %reduce-scatter.8.cloned.1.call-update) | async-done | bytes 262160 | tf_op jit(solution)/shard_map/reduce_scatter | solution.py:33
  (147 shorter events, 130.4 us)
Async XLA Ops:
  6.5 235.7 %reduce-scatter.4.cloned.1.call-start = ((), (), s32[]{:S(2)}) async-start(), calls=%async_computation.4 | async-start | bytes 4456448 | tf_op jit(solution)/shard_map/reduce_scatter | solution.py:33
  6.5 9.7 %collective-permute-start = (bf16[64,2048]{1,0:T(8,128)(2,1)}, bf16[64,2048]{1,0:T(8,128)(2,1)S(1)}, u32[]{:S(2)}, u32[]{:S(2)}) collective-permute-start(bf16[64,2048]{1,0:T(8,128)(2,1)} %param.15), channel_id=1, source_target_pairs={{0,1},{1,2},{2,3},{3,4},{4,5},{5,6},{6,7},{7,8},{8,9},{9,10},{10,1... | collective-permute-start | bytes 786440 | tf_op jit(solution)/shard_map/ppermute | solution.py:24
  16.3 8.5 %collective-permute-start.1 = (bf16[64,2048]{1,0:T(8,128)(2,1)S(1)}, bf16[64,2048]{1,0:T(8,128)(2,1)S(1)}, u32[]{:S(2)}, u32[]{:S(2)}) collective-permute-start(bf16[64,2048]{1,0:T(8,128)(2,1)S(1)} %collective-permute-done), channel_id=1, source_target_pairs={{0,1},{1,2},{2,3},{3,4},{4,5},{5,6},{6,7},{7,8},{8,9},{9,10},{10,1... | collective-permute-start | bytes 786440 | tf_op jit(solution)/shard_map/ppermute | solution.py:24
  24.8 8.5 %collective-permute-start.2 = (bf16[64,2048]{1,0:T(8,128)(2,1)S(1)}, bf16[64,2048]{1,0:T(8,128)(2,1)S(1)}, u32[]{:S(2)}, u32[]{:S(2)}) collective-permute-start(bf16[64,2048]{1,0:T(8,128)(2,1)S(1)} %collective-permute-done.1), channel_id=1, source_target_pairs={{0,1},{1,2},{2,3},{3,4},{4,5},{5,6},{6,7},{7,8},{8,9},{9,10},{10,1... | collective-permute-start | bytes 786440 | tf_op jit(solution)/shard_map/ppermute | solution.py:24
  33.3 8.5 %collective-permute-start.3 = (bf16[64,2048]{1,0:T(8,128)(2,1)S(1)}, bf16[64,2048]{1,0:T(8,128)(2,1)S(1)}, u32[]{:S(2)}, u32[]{:S(2)}) collective-permute-start(bf16[64,2048]{1,0:T(8,128)(2,1)S(1)} %collective-permute-done.2), channel_id=1, source_target_pairs={{0,1},{1,2},{2,3},{3,4},{4,5},{5,6},{6,7},{7,8},{8,9},{9,10},{10,1... | collective-permute-start | bytes 786440 | tf_op jit(solution)/shard_map/ppermute | solution.py:24
  51.7 8.5 %collective-permute-start.5 = (bf16[64,2048]{1,0:T(8,128)(2,1)S(1)}, bf16[64,2048]{1,0:T(8,128)(2,1)S(1)}, u32[]{:S(2)}, u32[]{:S(2)}) collective-permute-start(bf16[64,2048]{1,0:T(8,128)(2,1)S(1)} %collective-permute-done.4), channel_id=1, source_target_pairs={{0,1},{1,2},{2,3},{3,4},{4,5},{5,6},{6,7},{7,8},{8,9},{9,10},{10,1... | collective-permute-start | bytes 786440 | tf_op jit(solution)/shard_map/ppermute | solution.py:24
  60.9 8.5 %collective-permute-start.6 = (bf16[64,2048]{1,0:T(8,128)(2,1)S(1)}, bf16[64,2048]{1,0:T(8,128)(2,1)S(1)}, u32[]{:S(2)}, u32[]{:S(2)}) collective-permute-start(bf16[64,2048]{1,0:T(8,128)(2,1)S(1)} %collective-permute-done.5), channel_id=1, source_target_pairs={{0,1},{1,2},{2,3},{3,4},{4,5},{5,6},{6,7},{7,8},{8,9},{9,10},{10,1... | collective-permute-start | bytes 786440 | tf_op jit(solution)/shard_map/ppermute | solution.py:24
  70.1 8.5 %collective-permute-start.7 = (bf16[64,2048]{1,0:T(8,128)(2,1)S(1)}, bf16[64,2048]{1,0:T(8,128)(2,1)S(1)}, u32[]{:S(2)}, u32[]{:S(2)}) collective-permute-start(bf16[64,2048]{1,0:T(8,128)(2,1)S(1)} %collective-permute-done.6), channel_id=1, source_target_pairs={{0,1},{1,2},{2,3},{3,4},{4,5},{5,6},{6,7},{7,8},{8,9},{9,10},{10,1... | collective-permute-start | bytes 786440 | tf_op jit(solution)/shard_map/ppermute | solution.py:24
  79.2 8.5 %collective-permute-start.8 = (bf16[64,2048]{1,0:T(8,128)(2,1)S(1)}, bf16[64,2048]{1,0:T(8,128)(2,1)S(1)}, u32[]{:S(2)}, u32[]{:S(2)}) collective-permute-start(bf16[64,2048]{1,0:T(8,128)(2,1)S(1)} %collective-permute-done.7), channel_id=1, source_target_pairs={{0,1},{1,2},{2,3},{3,4},{4,5},{5,6},{6,7},{7,8},{8,9},{9,10},{10,1... | collective-permute-start | bytes 786440 | tf_op jit(solution)/shard_map/ppermute | solution.py:24
  88.4 8.5 %collective-permute-start.9 = (bf16[64,2048]{1,0:T(8,128)(2,1)S(1)}, bf16[64,2048]{1,0:T(8,128)(2,1)S(1)}, u32[]{:S(2)}, u32[]{:S(2)}) collective-permute-start(bf16[64,2048]{1,0:T(8,128)(2,1)S(1)} %collective-permute-done.8), channel_id=1, source_target_pairs={{0,1},{1,2},{2,3},{3,4},{4,5},{5,6},{6,7},{7,8},{8,9},{9,10},{10,1... | collective-permute-start | bytes 786440 | tf_op jit(solution)/shard_map/ppermute | solution.py:24
  116.0 8.5 %collective-permute-start.12 = (bf16[64,2048]{1,0:T(8,128)(2,1)S(1)}, bf16[64,2048]{1,0:T(8,128)(2,1)S(1)}, u32[]{:S(2)}, u32[]{:S(2)}) collective-permute-start(bf16[64,2048]{1,0:T(8,128)(2,1)S(1)} %collective-permute-done.11), channel_id=1, source_target_pairs={{0,1},{1,2},{2,3},{3,4},{4,5},{5,6},{6,7},{7,8},{8,9},{9,10},{10,1... | collective-permute-start | bytes 786440 | tf_op jit(solution)/shard_map/ppermute | solution.py:24
  124.5 8.6 %collective-permute-start.13 = (bf16[64,2048]{1,0:T(8,128)(2,1)S(1)}, bf16[64,2048]{1,0:T(8,128)(2,1)}, u32[]{:S(2)}, u32[]{:S(2)}) collective-permute-start(bf16[64,2048]{1,0:T(8,128)(2,1)S(1)} %collective-permute-done.12), channel_id=1, source_target_pairs={{0,1},{1,2},{2,3},{3,4},{4,5},{5,6},{6,7},{7,8},{8,9},{9,10},{10,1... | collective-permute-start | bytes 786440 | tf_op jit(solution)/shard_map/ppermute | solution.py:24
  133.1 19.4 %collective-permute-start.14 = (bf16[64,2048]{1,0:T(8,128)(2,1)}, bf16[64,2048]{1,0:T(8,128)(2,1)}, u32[]{:S(2)}, u32[]{:S(2)}) collective-permute-start(bf16[64,2048]{1,0:T(8,128)(2,1)} %collective-permute-done.13), channel_id=1, source_target_pairs={{0,1},{1,2},{2,3},{3,4},{4,5},{5,6},{6,7},{7,8},{8,9},{9,10},{10,1... | collective-permute-start | bytes 786440 | tf_op jit(solution)/shard_map/ppermute | solution.py:24
  171.0 167.3 %reduce-scatter.6.cloned.1.call-start = ((), (), s32[]{:S(2)}) async-start(), calls=%async_computation.5 | async-start | bytes 4456448 | tf_op jit(solution)/shard_map/reduce_scatter | solution.py:70
  265.8 281.5 %reduce-scatter.8.cloned.1.call-start = ((), (), s32[]{:S(2)}) async-start(), calls=%async_computation.6 | async-start | bytes 4456448 | tf_op jit(solution)/shard_map/reduce_scatter | solution.py:33
  339.4 8.5 %collective-permute-start.15 = (bf16[64,2048]{1,0:T(8,128)(2,1)S(1)}, bf16[64,2048]{1,0:T(8,128)(2,1)S(1)}, u32[]{:S(2)}, u32[]{:S(2)}) collective-permute-start(bf16[64,2048]{1,0:T(8,128)(2,1)S(1)} %fusion.25), channel_id=1, source_target_pairs={{0,1},{1,2},{2,3},{3,4},{4,5},{5,6},{6,7},{7,8},{8,9},{9,10},{10,1... | collective-permute-start | bytes 786440 | tf_op jit(solution)/shard_map/ppermute | solution.py:24
  348.0 8.5 %collective-permute-start.16 = (bf16[64,2048]{1,0:T(8,128)(2,1)S(1)}, bf16[64,2048]{1,0:T(8,128)(2,1)S(1)}, u32[]{:S(2)}, u32[]{:S(2)}) collective-permute-start(bf16[64,2048]{1,0:T(8,128)(2,1)S(1)} %collective-permute-done.15), channel_id=1, source_target_pairs={{0,1},{1,2},{2,3},{3,4},{4,5},{5,6},{6,7},{7,8},{8,9},{9,10},{10,1... | collective-permute-start | bytes 786440 | tf_op jit(solution)/shard_map/ppermute | solution.py:24
  356.5 8.5 %collective-permute-start.17 = (bf16[64,2048]{1,0:T(8,128)(2,1)S(1)}, bf16[64,2048]{1,0:T(8,128)(2,1)S(1)}, u32[]{:S(2)}, u32[]{:S(2)}) collective-permute-start(bf16[64,2048]{1,0:T(8,128)(2,1)S(1)} %collective-permute-done.16), channel_id=1, source_target_pairs={{0,1},{1,2},{2,3},{3,4},{4,5},{5,6},{6,7},{7,8},{8,9},{9,10},{10,1... | collective-permute-start | bytes 786440 | tf_op jit(solution)/shard_map/ppermute | solution.py:24
  365.0 8.5 %collective-permute-start.18 = (bf16[64,2048]{1,0:T(8,128)(2,1)S(1)}, bf16[64,2048]{1,0:T(8,128)(2,1)S(1)}, u32[]{:S(2)}, u32[]{:S(2)}) collective-permute-start(bf16[64,2048]{1,0:T(8,128)(2,1)S(1)} %collective-permute-done.17), channel_id=1, source_target_pairs={{0,1},{1,2},{2,3},{3,4},{4,5},{5,6},{6,7},{7,8},{8,9},{9,10},{10,1... | collective-permute-start | bytes 786440 | tf_op jit(solution)/shard_map/ppermute | solution.py:24
  398.9 8.5 %collective-permute-start.22 = (bf16[64,2048]{1,0:T(8,128)(2,1)S(1)}, bf16[64,2048]{1,0:T(8,128)(2,1)S(1)}, u32[]{:S(2)}, u32[]{:S(2)}) collective-permute-start(bf16[64,2048]{1,0:T(8,128)(2,1)S(1)} %collective-permute-done.21), channel_id=1, source_target_pairs={{0,1},{1,2},{2,3},{3,4},{4,5},{5,6},{6,7},{7,8},{8,9},{9,10},{10,1... | collective-permute-start | bytes 786440 | tf_op jit(solution)/shard_map/ppermute | solution.py:24
  407.4 8.5 %collective-permute-start.23 = (bf16[64,2048]{1,0:T(8,128)(2,1)S(1)}, bf16[64,2048]{1,0:T(8,128)(2,1)S(1)}, u32[]{:S(2)}, u32[]{:S(2)}) collective-permute-start(bf16[64,2048]{1,0:T(8,128)(2,1)S(1)} %collective-permute-done.22), channel_id=1, source_target_pairs={{0,1},{1,2},{2,3},{3,4},{4,5},{5,6},{6,7},{7,8},{8,9},{9,10},{10,1... | collective-permute-start | bytes 786440 | tf_op jit(solution)/shard_map/ppermute | solution.py:24
  415.9 8.5 %collective-permute-start.24 = (bf16[64,2048]{1,0:T(8,128)(2,1)S(1)}, bf16[64,2048]{1,0:T(8,128)(2,1)S(1)}, u32[]{:S(2)}, u32[]{:S(2)}) collective-permute-start(bf16[64,2048]{1,0:T(8,128)(2,1)S(1)} %collective-permute-done.23), channel_id=1, source_target_pairs={{0,1},{1,2},{2,3},{3,4},{4,5},{5,6},{6,7},{7,8},{8,9},{9,10},{10,1... | collective-permute-start | bytes 786440 | tf_op jit(solution)/shard_map/ppermute | solution.py:24
  424.4 8.5 %collective-permute-start.25 = (bf16[64,2048]{1,0:T(8,128)(2,1)S(1)}, bf16[64,2048]{1,0:T(8,128)(2,1)S(1)}, u32[]{:S(2)}, u32[]{:S(2)}) collective-permute-start(bf16[64,2048]{1,0:T(8,128)(2,1)S(1)} %collective-permute-done.24), channel_id=1, source_target_pairs={{0,1},{1,2},{2,3},{3,4},{4,5},{5,6},{6,7},{7,8},{8,9},{9,10},{10,1... | collective-permute-start | bytes 786440 | tf_op jit(solution)/shard_map/ppermute | solution.py:24
  432.9 8.5 %collective-permute-start.26 = (bf16[64,2048]{1,0:T(8,128)(2,1)S(1)}, bf16[64,2048]{1,0:T(8,128)(2,1)S(1)}, u32[]{:S(2)}, u32[]{:S(2)}) collective-permute-start(bf16[64,2048]{1,0:T(8,128)(2,1)S(1)} %collective-permute-done.25), channel_id=1, source_target_pairs={{0,1},{1,2},{2,3},{3,4},{4,5},{5,6},{6,7},{7,8},{8,9},{9,10},{10,1... | collective-permute-start | bytes 786440 | tf_op jit(solution)/shard_map/ppermute | solution.py:24
  (33 other events, 626.1 us)
Sparse Core Ops, SparseCore 0:
  171.1 71.1 reduce-scatter.3
  265.9 72.3 reduce-scatter.5
  477.2 69.9 reduce-scatter.7
